TPU v7x, 512 devices: a whole 4x4x16 slice. The times are simulated.
512 devices in a mesh: feat: 8 (over z_lo), lat: 64 (over y, z_hi, x, core).
Axes of the slice: x: 4, y: 4, z: 16 (z_hi: 2, z_lo: 8; z = z_hi * 8 + z_lo), core: 2. Of those that a mesh axis runs over, the one named last changes fastest.
Arguments:
- acts: bfloat16 [2, 512, 4096], P(None, 'lat', 'feat'), may hold values from -6 to 6
- weight: bfloat16 [2, 4096, 65536], P(None, 'feat', 'lat'), may hold values from -0.0625 to 0.0625
- enc_bias: float32 [65536], P('lat'), may hold values from -1 to 0.5
- dec_bias: float32 [2, 4096], P(None, 'feat'), may hold values from -1 to 1
Outputs:
- grad_weight: bfloat16 [2, 4096, 65536], P(None, 'feat', 'lat')
- grad_enc_bias: float32 [65536], P('lat')
- grad_dec_bias: float32 [2, 4096], P(None, 'feat')
All inputs are finite; a program needn't handle non-finite values.
Results may differ from a plain program's by a relative error of at most 0.0085.
Values may be sent and summed in bfloat16 or wider, within the bound.
A program may use at most 64 MiB of HBM per device.

v0:
```python
import math

import jax
import jax.numpy as jnp
from jax import lax
from jax.sharding import Mesh
from jax.sharding import PartitionSpec as P

LAT = ("lat_0", "lat_1", "lat_2", "lat_3")


def in_blocks(shard, dim, count):
    dims = shard.shape
    blocks = shard.reshape(*dims[:dim], count, dims[dim] // count, *dims[dim + 1 :])
    return jnp.moveaxis(blocks, dim, 0)


def summed_on_arrival(shard, axis, dim):
    blocks = in_blocks(shard, dim, lax.axis_size(axis))
    arrived = lax.all_to_all(blocks, axis, split_axis=0, concat_axis=0, tiled=True)
    return arrived.astype(jnp.float32).sum(axis=0)


def in_order(blocks, dim):
    dims = list(blocks.shape[1:])
    dims[dim] *= blocks.shape[0]
    return jnp.moveaxis(blocks, 0, dim).reshape(dims)


def from_everyone(shard, axis):
    copies = jnp.broadcast_to(shard, (lax.axis_size(axis), *shard.shape))
    return lax.all_to_all(copies, axis, split_axis=0, concat_axis=0, tiled=True)


def gathered_copies(shard, axis, dim):
    return in_order(from_everyone(shard, axis), dim)


def sum_at_owner(shard, axis, dim):
    count = lax.axis_size(axis)
    blocks = lax.all_to_all(in_blocks(shard, dim, count), axis, 0, 0, tiled=True)
    return jnp.sum(blocks, axis=0)


def sum_by_axis(shard, axes, dim):
    far, near = axes
    blocks = in_blocks(shard, dim, lax.axis_size(far))
    nearer = sum_at_owner(blocks, near, dim + 1)
    arrived = lax.all_to_all(nearer, far, split_axis=0, concat_axis=0, tiled=True)
    return arrived.sum(axis=0)


def filled_up(lines, count):
    spare = -len(lines) % count
    return jnp.pad(lines, [(0, spare)] + [(0, 0)] * (lines.ndim - 1))


def gathered_by_axis(shard, axes, dim):
    far, near = axes
    blocks = from_everyone(from_everyone(shard, far), near)
    return in_order(blocks.swapaxes(0, 1).reshape(-1, *shard.shape), dim)


def nested_sum(shard, axes):
    lines = shard.reshape(-1, shard.shape[-1])
    own = sum_by_axis(filled_up(lines, lax.axis_size(axes[0]) * lax.axis_size(axes[1])), axes, 0)
    whole = gathered_by_axis(own, axes, 0)
    return whole[: len(lines)].reshape(shard.shape)


def taken_together(shard, axis):
    everything = from_everyone(shard, axis)
    return jnp.sum(everything, axis=0)


def channel_terms(left, right):
    first = jnp.dot(left[0], right[0], preferred_element_type=jnp.float32)
    return first + jnp.dot(left[1], right[1], preferred_element_type=jnp.float32)


def on_device(acts, weight, enc_bias, dec_bias):
    width = weight.shape[1] * lax.axis_size("feat")
    lats = weight.shape[2] * lax.axis_size(LAT)
    scale = math.sqrt(2.0 * width / lats)
    whole_rows = lax.all_gather(acts, LAT, axis=1, tiled=True)
    partial_value = channel_terms(whole_rows, weight)
    pre_share = summed_on_arrival(partial_value.astype(jnp.bfloat16), "feat", 0) + enc_bias
    act_share = jax.nn.softplus(pre_share).astype(jnp.bfloat16)
    latents = gathered_copies(act_share, "feat", 0)
    recon_terms = jnp.einsum("rl,mdl->mrd", latents, weight, preferred_element_type=jnp.float32)
    summed = nested_sum(recon_terms, (("lat_0", "lat_1", "lat_2"), "lat_3"))
    resid = scale * summed + dec_bias[:, None, :] - whole_rows.astype(jnp.float32)
    grad_dec_bias = jnp.sum(resid, axis=1)
    resid_rows = resid.astype(jnp.bfloat16)
    backed = channel_terms(resid_rows, weight)
    back_part = summed_on_arrival(backed.astype(jnp.bfloat16), "feat", 0)
    grad_share = scale * back_part * jax.nn.sigmoid(pre_share)
    grad_enc_bias = taken_together(jnp.sum(grad_share, axis=0), "feat")
    grad_pre_b = gathered_copies(grad_share.astype(jnp.bfloat16), "feat", 0)
    enc_term = jnp.einsum("mrd,rl->mdl", whole_rows, grad_pre_b, preferred_element_type=jnp.float32)
    dec_term = jnp.einsum("mrd,rl->mdl", resid_rows, latents, preferred_element_type=jnp.float32)
    grad_weight = (enc_term + scale * dec_term).astype(jnp.bfloat16)
    return (grad_weight, grad_enc_bias, grad_dec_bias)


def solution(mesh):
    torus = Mesh(
        mesh.devices.reshape(mesh.shape["feat"], 4, 2, 4, 2),
        ("feat", "lat_0", "lat_1", "lat_2", "lat_3"),
    )
    in_specs = (P(None, LAT, "feat"), P(None, "feat", LAT), P(LAT), P(None, "feat"))
    out_specs = (P(None, "feat", LAT), P(LAT), P(None, "feat"))
    return jax.shard_map(
        on_device, mesh=torus, in_specs=in_specs, out_specs=out_specs, check_vma=False
    )
```

profile of v0, /device:TPU:2, one launch (start us, length us, event | category | flops | bytes accessed | tf_op | source)
XLA Modules:
  0.0 509.9 jit_solution(4687224585062646519)
XLA Ops:
  7.2 0.0 copy-start.1
  7.2 0.0 all-gather.2.cloned.1.call-start
  7.2 0.7 all-gather.2.cloned.1.call-update
  7.9 110.8 %all-gather.2.cloned.1.call-done = bf16[2,512,512]{2,1,0:T(8,128)(2,1)} async-done(((bf16[2,8,512]{2,1,0:T(8,128)(2,1)}), bf16[2,512,512]{2,1,0:T(8,128)(2,1)}) %all-gather.2.cloned.1.call-update) | async-done | bytes 1048592 | tf_op jit(solution)/shard_map/all_gather | solution.py:85
  118.8 0.0 copy-start
  118.8 2.2 fusion.7
  120.9 0.0 copy-done.1
  121.0 0.0 copy-done
  121.0 0.7 add_convert_fusion.1
  121.7 0.0 copy-start.5
  121.7 54.3 %all_to_all.46 = bf16[8,64,1024]{2,1,0:T(8,128)(2,1)S(1)} all-to-all(bf16[8,64,1024]{2,1,0:T(8,128)(2,1)S(1)} %bitcast.52), channel_id=1, replica_groups=mesh['feat'=8,'lat_0'=4,'lat_1'=2,'lat_2'=4,'lat_3'=2] {'feat'}, dimensions={0} | all-to-all | bytes 2097152 | tf_op jit(solution)/shard_map/all_to_all | solution.py:20
  176.0 0.2 convert_reduce_fusion.1
  176.2 0.0 copy-done.5
  176.2 0.2 fusion.13
  176.3 0.1 broadcast_in_dim.17
  176.5 55.2 %all_to_all.47 = bf16[8,64,1024]{2,1,0:T(8,128)(2,1)S(1)} all-to-all(bf16[8,64,1024]{2,1,0:T(8,128)(2,1)S(1)} %broadcast_in_dim.17), channel_id=1, replica_groups=mesh['feat'=8,'lat_0'=4,'lat_1'=2,'lat_2'=4,'lat_3'=2] {'feat'}, dimensions={0} | all-to-all | bytes 2097152 | tf_op jit(solution)/shard_map/all_to_all | solution.py:32
  231.7 0.0 copy-start.3
  231.7 1.3 fusion.15
  233.0 0.0 copy-done.3
  233.0 0.3 copy.40
  233.3 5.4 %all_to_all.48 = f32[2,32,16,512]{3,2,1,0:T(8,128)S(1)} all-to-all(f32[2,32,16,512]{3,2,1,0:T(8,128)S(1)} %bitcast.50), channel_id=1, replica_groups=mesh['feat'=8,'lat_0'=4,'lat_1'=2,'lat_2'=4,'lat_3'=2] {'lat_3'}, dimensions={0} | all-to-all | bytes 4194304 | tf_op jit(solution)/shard_map/all_to_all | solution.py:41
  238.7 1.3 reduce_sum.64
  239.9 60.7 %all_to_all.49 = f32[32,16,512]{2,1,0:T(8,128)S(1)} all-to-all(f32[32,16,512]{2,1,0:T(8,128)} %reduce_sum.64), channel_id=1, replica_groups=mesh['feat'=8,'lat_0'=4,'lat_1'=2,'lat_2'=4,'lat_3'=2] {'lat_0','lat_1',..., dimensions={0} | all-to-all | bytes 2097152 | tf_op jit(solution)/shard_map/all_to_all | solution.py:49
  300.6 0.1 reduce_sum.65
  300.7 0.1 broadcast_in_dim.18
  300.8 50.3 %all_to_all.50 = f32[32,16,512]{2,1,0:T(8,128)S(1)} all-to-all(f32[32,16,512]{2,1,0:T(8,128)S(1)} %broadcast_in_dim.18), channel_id=1, replica_groups=mesh['feat'=8,'lat_0'=4,'lat_1'=2,'lat_2'=4,'lat_3'=2] {'lat_0','lat_1',..., dimensions={0} | all-to-all | bytes 2097152 | tf_op jit(solution)/shard_map/all_to_all | solution.py:32
  351.1 0.3 broadcast_in_dim.19
  351.3 5.4 %all_to_all.51 = f32[2,32,16,512]{3,2,1,0:T(8,128)S(1)} all-to-all(f32[2,32,16,512]{3,2,1,0:T(8,128)S(1)} %broadcast_in_dim.19), channel_id=1, replica_groups=mesh['feat'=8,'lat_0'=4,'lat_1'=2,'lat_2'=4,'lat_3'=2] {'lat_3'}, dimensions={0} | all-to-all | bytes 4194304 | tf_op jit(solution)/shard_map/all_to_all | solution.py:32
  356.8 0.2 multiply_bitcast_fusion
  357.0 0.0 copy-start.6
  357.0 0.3 copy.28
  357.3 0.4 copy-done.6
  357.7 1.0 fusion.1
  358.7 0.6 copy-done.2
  359.3 0.7 fusion.5
  360.0 0.7 add_convert_fusion
  360.7 65.0 %all_to_all.52 = bf16[8,64,1024]{2,1,0:T(8,128)(2,1)S(1)} all-to-all(bf16[8,64,1024]{2,1,0:T(8,128)(2,1)S(1)} %bitcast.53), channel_id=1, replica_groups=mesh['feat'=8,'lat_0'=4,'lat_1'=2,'lat_2'=4,'lat_3'=2] {'feat'}, dimensions={0} | all-to-all | bytes 2097152 | tf_op jit(solution)/shard_map/all_to_all | solution.py:20
  425.7 0.2 convert_reduce_fusion
  425.9 0.1 fusion.14
  426.0 14.7 %all_to_all.53 = f32[8,1,1024]{2,1,0:T(1,128)S(1)} all-to-all(f32[8,1,1024]{2,1,0:T(1,128)S(1)} %broadcast_in_dim.21), channel_id=1, replica_groups=mesh['feat'=8,'lat_0'=4,'lat_1'=2,'lat_2'=4,'lat_3'=2] {'feat'}, dimensions={0} | all-to-all | bytes 65536 | tf_op jit(solution)/shard_map/all_to_all | solution.py:32
  440.7 1.1 broadcast_in_dim.20
  441.8 3.6 all-to-all-start.7
  445.4 0.6 reduce_sum.68
  446.0 49.1 %all-to-all-done.7 = bf16[8,64,1024]{2,1,0:T(8,128)(2,1)S(1)} async-done(((bf16[8,64,1024]{2,1,0:T(8,128)(2,1)}), bf16[8,64,1024]{2,1,0:T(8,128)(2,1)S(1)}, u32[]{:S(2)}, u32[]{:S(2)}) %all-to-all-start.7) | async-done | bytes 1048608 | tf_op jit(solution)/shard_map/all_to_all | solution.py:32
  495.1 1.3 fusion.16
  496.4 0.0 copy-done.4
  496.4 2.8 fusion
  499.1 3.9 copy.33
  (3 shorter events, 0.0 us)
Async XLA Ops:
  7.2 113.8 %copy-start.1 = (bf16[2,512,1024]{2,1,0:T(8,128)(2,1)S(1)}, bf16[2,512,1024]{2,1,0:T(8,128)(2,1)}, u32[]{:S(2)}) copy-start(bf16[2,512,1024]{2,1,0:T(8,128)(2,1)} %param.5) | copy-start | bytes 6291460
  7.2 111.6 %all-gather.2.cloned.1.call-start = ((), (), s32[]{:S(2)}) async-start(), calls=%async_computation.9 | async-start | bytes 1064960 | tf_op jit(solution)/shard_map/all_gather | solution.py:85
  118.8 2.2 copy-start
  121.7 54.5 %copy-start.5 = (f32[1024]{0:T(1024)S(1)}, f32[1024]{0:T(1024)}, u32[]{:S(2)}) copy-start(f32[1024]{0:T(1024)} %param.6) | copy-start | bytes 12292
  231.7 1.3 copy-start.3
  357.0 0.7 copy-start.6
  357.7 1.6 copy-start.2
  441.8 53.3 %all-to-all-start.7 = ((bf16[8,64,1024]{2,1,0:T(8,128)(2,1)}), bf16[8,64,1024]{2,1,0:T(8,128)(2,1)S(1)}, u32[]{:S(2)}, u32[]{:S(2)}) async-start(bf16[8,64,1024]{2,1,0:T(8,128)(2,1)} %broadcast_in_dim.20), calls=%async_computation.7 | async-start | bytes 2097152 | tf_op jit(solution)/shard_map/all_to_all | solution.py:32
  495.1 1.3 copy-start.4
Sparse Core Ops, SparseCore 0:
  12.2 106.4 all-gather.1
where the time goes:
time: 511 us; the launch traced here: 510 us
  blocking collectives  311 us (61%)
  waiting for transfers between devices  161 us (32%)
  between operations  14.2 us (3%)
  matrix products  9.68 us (2%)
  local copies, waits for them, and re-layouts  7.09 us (1%)
    all_to_all x4, blocking collectives, from_everyone(): return lax.all_to_all(copies, axis, split_axis=0, concat_axis=0, tiled=True)  126 us
    all_to_all x2, blocking collectives, summed_on_arrival(): lax.all_to_all(blocks, axis, split_axis=0, concat_axis=0, tiled=True)  119 us
    all_gather x1, waiting for transfers between devices, on_device(): whole_rows = lax.all_gather(acts, LAT, axis=1, tiled=True)  111 us
    all_to_all x1, blocking collectives, sum_by_axis(): lax.all_to_all(nearer, far, split_axis=0, concat_axis=0, tiled=True)  60.7 us
    all_to_all x1, waiting for transfers between devices, from_everyone(): return lax.all_to_all(copies, axis, split_axis=0, concat_axis=0, tiled=True)  49.1 us
  transfers between devices with their start and end apart: 2, of which 2 were waited for; matrix products, arithmetic and copies ran while one was open for 0% of the time, Pallas kernels for 0%

commit v1 on v0

v1 whole, which is shorter than its diff:
```python
import functools
import math

import jax
import jax.numpy as jnp
from jax import lax
from jax.experimental import pallas as pl
from jax.experimental.pallas import tpu as pltpu
from jax.sharding import Mesh
from jax.sharding import PartitionSpec as P

LAT = ("lat_0", "lat_1", "lat_2", "lat_3")
AXES = ("feat", *LAT)
BF16, F32 = jnp.bfloat16, jnp.float32
TILE = 16
SKEW = 5


def chain_kernel(
    sizes, scale, a_ref, w_hbm, eb_ref, db_ref, gw_ref, geb_ref, gdb_ref,
    w_ref, abuf, xs, prod, sig, lats, grads, res, sr, ss, tl, ts, sr2, ss2, tl2, ts2,
    half_out, half_in, half_own, part_out, part_in, pair_out, pair_in, acc, gacc, gebuf,
    w_sem, h_sem, xy_sem, core_sem, line_sem, line2_sem, geb_send, geb_recv,
):
    nf, ny, _, nx, _ = sizes
    nq = ny * nx
    nt = 2 * nq
    width, nlat = w_ref.shape[1], w_ref.shape[2]
    f, y, h, x, c = (lax.axis_index(name) for name in AXES)
    q = y * nx + x
    mine, base, other_base = c * nq + q, c * nq, (1 - c) * nq
    mid = (nf - 1) // 2
    partner, sibling = (f, y, 1 - h, x, c), (f, y, h, x, 1 - c)
    after, before = (jnp.minimum(f + 1, nf - 1), y, h, x, c), (jnp.maximum(f - 1, 0), y, h, x, c)
    offsets = [(dy, dx) for dy in range(ny) for dx in range(nx) if dy or dx]

    def at_offset(dy, dx):
        return lax.rem(y + dy + ny, ny), lax.rem(x + dx + nx, nx)

    def remote(src, dst, send, recv, to):
        return pltpu.make_async_remote_copy(
            src_ref=src, dst_ref=dst, send_sem=send, recv_sem=recv,
            device_id=to, device_id_type=pl.DeviceIdType.MESH,
        )

    w_copy = pltpu.make_async_copy(w_hbm, w_ref, w_sem)
    w_copy.start()

    barrier = pltpu.get_barrier_semaphore()

    def greet(to):
        pl.semaphore_signal(barrier, inc=1, device_id=to, device_id_type=pl.DeviceIdType.MESH)

    greet(partner)
    greet(sibling)
    for dy, dx in offsets:
        py, px = at_offset(dy, dx)
        greet((f, py, h, px, c))

    @pl.when(f > 0)
    def _():
        greet(before)

    @pl.when(f < nf - 1)
    def _():
        greet(after)

    @pl.when(f != mid)
    def _():
        greet((mid, y, h, x, c))

    beside = (f > 0).astype(jnp.int32) + (f < nf - 1).astype(jnp.int32)
    listeners = (nf - 1) * (f == mid).astype(jnp.int32)
    pl.semaphore_wait(barrier, 2 + len(offsets) + beside + listeners)

    def swap_along_z(src, dst, at):
        copy = remote(src, dst, h_sem.at[0, at], h_sem.at[1, at], partner)
        copy.start()
        copy.wait()

    def gathered(buf, at):
        sends, passed = [], []

        def pass_on(tile, source):
            copy = remote(
                buf.at[tile], buf.at[tile], core_sem.at[0, at, source], core_sem.at[1, at, source], sibling
            )
            copy.start()
            passed.append(copy)

        for number, (dy, dx) in enumerate(offsets):
            py, px = at_offset(dy, dx)
            copy = remote(
                buf.at[mine], buf.at[mine], xy_sem.at[0, at, number], xy_sem.at[1, at, q], (f, py, h, px, c)
            )
            copy.start()
            sends.append(copy)
        pass_on(mine, q)
        for dy, dx in offsets:
            py, px = at_offset(-dy, -dx)
            source = py * nx + px
            remote(
                buf.at[mine], buf.at[base + source], xy_sem.at[0, at, 0], xy_sem.at[1, at, source], sibling
            ).wait_recv()
            pass_on(base + source, source)
        for copy in sends + passed:
            copy.wait_send()
        for source in range(nq):
            remote(
                buf.at[mine], buf.at[other_base + source], core_sem.at[0, at, 0], core_sem.at[1, at, source], sibling
            ).wait_recv()

    def products(left):
        per = min(16, nt)
        columns = 256

        @pl.loop(0, nt // per)
        def _(group):
            tiles = pl.ds(group * per, per)

            @pl.loop(0, nlat // columns)
            def _(block):
                cols = pl.ds(pl.multiple_of(block * columns, columns), columns)
                total = jnp.dot(
                    left[tiles, 0].reshape(per * TILE, width), w_ref[0, :, cols], preferred_element_type=F32
                )
                total = total + jnp.dot(
                    left[tiles, 1].reshape(per * TILE, width), w_ref[1, :, cols], preferred_element_type=F32
                )
                prod[tiles, :, cols] = total.reshape(per, TILE, columns)

    def chained(right_in, right_out, left_in, left_out, sems, on_total, on_step):
        last = nf - 1

        @pl.when(f == 0)
        def _():
            right_in[...] = jnp.zeros_like(right_in)

        @pl.when(f == last)
        def _():
            left_in[...] = jnp.zeros_like(left_in)

        def to_right(k):
            return remote(right_out.at[k], right_in.at[k], sems.at[0, k], sems.at[1, k], after)

        def to_left(k):
            return remote(left_out.at[k], left_in.at[k], sems.at[2, k], sems.at[3, k], before)

        lag = jnp.maximum(f, last - f)

        @pl.loop(0, nt + SKEW * last)
        def _(step):
            right, left, done = step - SKEW * f, step - SKEW * (last - f), step - SKEW * lag

            @pl.when((right >= 0) & (right < nt))
            def _():
                @pl.when(f > 0)
                def _():
                    to_right(right).wait_recv()

                @pl.when(f < last)
                def _():
                    right_out[right] = (prod[right] + right_in[right].astype(F32)).astype(BF16)
                    to_right(right).start()

            @pl.when((left >= 0) & (left < nt))
            def _():
                @pl.when(f < last)
                def _():
                    to_left(left).wait_recv()

                @pl.when(f > 0)
                def _():
                    left_out[left] = (prod[left] + left_in[left].astype(F32)).astype(BF16)
                    to_left(left).start()

            @pl.when((done >= 0) & (done < nt))
            def _():
                on_total(done, prod[done] + right_in[done].astype(F32) + left_in[done].astype(F32))

            on_step(step)

        @pl.loop(0, nt)
        def _(k):
            @pl.when(f < last)
            def _():
                to_right(k).wait_send()

            @pl.when(f > 0)
            def _():
                to_left(k).wait_send()

    swap_along_z(a_ref, abuf, 0)
    own, far = a_ref[...].astype(F32), abuf[...].astype(F32)
    low, high = jnp.where(h == 0, own, far), jnp.where(h == 0, far, own)
    rows = TILE // 2
    for m in range(2):
        part = slice(m * rows, (m + 1) * rows)
        xs[mine, m] = jnp.concatenate([low[part], high[part]], axis=0).astype(BF16)
    gathered(xs, 0)

    w_copy.wait()
    products(xs)

    def activate(k, total):
        pre = total + eb_ref[...]
        fall = jnp.exp(-jnp.abs(pre))
        lats[k] = (jnp.maximum(pre, 0.0) + jnp.log1p(fall)).astype(BF16)
        sig[k] = jnp.where(pre >= 0, 1.0, fall) / (1.0 + fall)

    chained(sr, ss, tl, ts, line_sem, activate, lambda step: None)

    per = min(8, nq)

    def terms(tile, m):
        return lax.dot_general(
            lats[pl.ds(tile, per)].reshape(per * TILE, nlat), w_ref[m],
            (((1,), (1,)), ((), ())), preferred_element_type=F32,
        ).reshape(per, TILE, width)

    @pl.loop(0, nq // per)
    def _(group):
        for m in range(2):
            half_out[pl.ds(group * per, per), m] = terms(other_base + group * per, m).astype(BF16)

    half_copy = remote(half_out, half_in, h_sem.at[0, 2], h_sem.at[1, 2], sibling)
    half_copy.start()

    @pl.loop(0, nq // per)
    def _(group):
        for m in range(2):
            half_own[pl.ds(group * per, per), m] = terms(base + group * per, m)

    half_copy.wait()
    sends = []
    for number, (dy, dx) in enumerate(offsets):
        py, px = at_offset(dy, dx)
        owner = py * nx + px
        part_out[number] = (half_own[owner] + half_in[owner].astype(F32)).astype(BF16)
        copy = remote(
            part_out.at[number], part_in.at[number], xy_sem.at[0, 2, number], xy_sem.at[1, 2, number], (f, py, h, px, c)
        )
        copy.start()
        sends.append(copy)
    total = half_own[q] + half_in[q].astype(F32)
    for number, copy in enumerate(sends):
        copy.wait_recv()
        total = total + part_in[number].astype(F32)
    pair_out[...] = total.astype(BF16)
    swap_along_z(pair_out, pair_in, 1)
    summed = pair_out[...].astype(F32) + pair_in[...].astype(F32)
    res[mine] = (scale * summed + db_ref[...] - xs[mine].astype(F32)).astype(BF16)
    gathered(res, 1)
    for copy in sends:
        copy.wait_send()

    products(res)
    gacc[...] = jnp.zeros_like(gacc)
    channels, columns = 128, 256
    across = nlat // columns
    along = width // channels

    def blocks_of(number):
        chan = pl.ds(pl.multiple_of(lax.rem(number // across, along) * channels, channels), channels)
        cols = pl.ds(pl.multiple_of(lax.rem(number, across) * columns, columns), columns)
        return number // (across * along), chan, cols

    def over_rows(left, m, chan, right, cols):
        return lax.dot_general(
            left[:, m, :, chan].reshape(nt * TILE, channels), right[:, :, cols].reshape(nt * TILE, columns),
            (((0,), (0,)), ((), ())), preferred_element_type=F32,
        )

    def dec_block(step):
        @pl.when(step < 2 * across * along)
        def _():
            m, chan, cols = blocks_of(step)
            acc[m, chan, cols] = scale * over_rows(res, m, chan, lats, cols)

    def finish(k, total):
        grad = scale * total * sig[k]
        grads[k] = grad.astype(BF16)
        gacc[...] += grad

    chained(sr2, ss2, tl2, ts2, line2_sem, finish, dec_block)

    first = 2 * across * along - (nt + SKEW * (nf - 1))
    if first > 0:
        @pl.loop(nt + SKEW * (nf - 1), 2 * across * along)
        def _(number):
            dec_block(number)

    def to_chip(ahead):
        return remote(
            gebuf, gebuf, geb_send.at[ahead], geb_recv.at[0], (lax.rem(mid + ahead, nf), y, h, x, c)
        )

    @pl.when(f == mid)
    def _():
        gebuf[...] = jnp.broadcast_to(jnp.sum(gacc[...], axis=0, keepdims=True), gebuf.shape)
        for ahead in range(1, nf):
            to_chip(ahead).start()

    gdb_ref[...] = jnp.sum(jnp.sum(res[...].astype(F32), axis=0), axis=1, keepdims=True)

    @pl.loop(0, 2 * across * along)
    def _(number):
        m, chan, cols = blocks_of(number)
        gw_ref[m, chan, cols] = (over_rows(xs, m, chan, grads, cols) + acc[m, chan, cols]).astype(BF16)

    @pl.when(f == mid)
    def _():
        for ahead in range(1, nf):
            to_chip(ahead).wait_send()

    @pl.when(f != mid)
    def _():
        to_chip(1).wait_recv()

    geb_ref[...] = gebuf[0:1]


def on_device(sizes, acts, weight, enc_bias, dec_bias):
    nf, ny, nh, nx, nc = sizes
    lat_count = ny * nh * nx * nc
    _, width, nlat = weight.shape
    scale = math.sqrt(2.0 * (width * nf) / (nlat * lat_count))
    nq = ny * nx
    nt = 2 * nq
    vmem = pltpu.VMEM
    tiles = vmem((nt, 2, TILE, width), BF16)
    chunk = vmem((nt, TILE, nlat), BF16)
    wide = vmem((nt, TILE, nlat), F32)
    half = vmem((nq, 2, TILE, width), BF16)
    pair = vmem((2, TILE, width), BF16)
    parts = vmem((max(nq - 1, 1), 2, TILE, width), BF16)
    dma = pltpu.SemaphoreType.DMA
    whole = pl.BlockSpec(memory_space=pltpu.VMEM)
    grad_weight, grad_enc, grad_dec = pl.pallas_call(
        functools.partial(chain_kernel, sizes, scale),
        out_shape=(
            jax.ShapeDtypeStruct((2, width, nlat), BF16),
            jax.ShapeDtypeStruct((1, nlat), F32),
            jax.ShapeDtypeStruct((2, 1, width), F32),
        ),
        in_specs=[whole, pl.BlockSpec(memory_space=pl.ANY), whole, whole],
        out_specs=(whole, whole, whole),
        scratch_shapes=[
            vmem((2, width, nlat), BF16), vmem((TILE, width), BF16),
            tiles, wide, wide, chunk, chunk, tiles,
            *([chunk] * 8),
            half, half, vmem((nq, 2, TILE, width), F32), parts, parts, pair, pair,
            vmem((2, width, nlat), F32), vmem((TILE, nlat), F32), vmem((8, nlat), F32),
            dma, dma((2, 3)), dma((2, 3, max(nq, 1))), dma((2, 2, nq)), dma((4, nt)), dma((4, nt)),
            dma((nf,)), dma((1,)),
        ],
        compiler_params=pltpu.CompilerParams(
            collective_id=0, has_side_effects=True, vmem_limit_bytes=60 * 1024 * 1024
        ),
        name="crosscoder_step",
    )(acts.reshape(TILE, width), weight, enc_bias.reshape(1, nlat), dec_bias.reshape(2, 1, width))
    return grad_weight, grad_enc.reshape(nlat), grad_dec.reshape(2, width)


def solution(mesh):
    shape = dict(mesh.shape)
    if shape["lat"] == 64:
        sizes = (shape["feat"], 4, 2, 4, 2)
    else:
        sizes = (shape["feat"], 1, 2, shape["lat"] // 4, 2)
    torus = Mesh(mesh.devices.reshape(sizes), AXES)
    in_specs = (P(None, LAT, "feat"), P(None, "feat", LAT), P(LAT), P(None, "feat"))
    out_specs = (P(None, "feat", LAT), P(LAT), P(None, "feat"))
    return jax.shard_map(
        functools.partial(on_device, sizes),
        mesh=torus, in_specs=in_specs, out_specs=out_specs, check_vma=False,
    )
```

time: 511 us -> 180 us (0.35)
  the two profiles are of different devices: /device:TPU:2 before, /device:TPU:1 now
where the time goes in v1:
time: 180 us; the launch traced here: 179 us
  Pallas kernels  172 us (96%)
  local copies, waits for them, and re-layouts  6.23 us (3%)
    pallas_call x1, Pallas kernels, on_device(): pl.pallas_call(functools.partial(chain_kernel, sizes, scale), out_shape=(...  172 us
    unnamed x5, local copies, waits for them, and re-layouts  4.95 us

profile of v1, /device:TPU:1, one launch (start us, length us, event | category | flops | bytes accessed | tf_op | source)
XLA Modules:
  0.0 179.3 jit_solution(6126472265046289513)
XLA Ops:
  0.6 1.3 reshape.23.db_ref
  1.9 172.4 %crosscoder_step.1 = (bf16[2,512,1024]{2,1,0:T(8,128)(2,1)}, f32[1,1024]{1,0:T(1,128)}, f32[2,1,512]{2,1,0:T(1,128)}) custom-call(bf16[16,512]{1,0:T(8,128)(2,1)} %bitcast.6, bf16[2,512,1024]{2,1,0:T(8,128)(2,1)} %w_hbm.1, f32[1,1024]{1,0:T(1,128)} %bitcast.7, f32[2,1,512]{2,1,0:T(1,128)} %reshape.23.db_ref), custom_call_target="tpu_custom_call" | custom-call | tf_op jit(solution)/shard_map/crosscoder_step/pallas_call | solution.py:339
  174.3 1.3 copy.9
  175.6 0.0 copy-start
  175.6 3.1 %copy.12 = bf16[2,512,1024]{2,1,0:T(8,128)(2,1)} copy(bf16[2,512,1024]{2,1,0:T(8,128)(2,1)} %get-tuple-element.12) | data formatting | bytes 4194304
  178.7 0.0 copy-done
  178.7 0.6 copy.13
Async XLA Ops:
  175.6 3.1 %copy-start = (f32[1,1024]{1,0:T(1,128)S(1)}, f32[1,1024]{1,0:T(1,128)}, u32[]{:S(2)}) copy-start(f32[1,1024]{1,0:T(1,128)} %get-tuple-element.7) | copy-start | bytes 12292

commit v2 on v1

v2 whole, which is shorter than its diff:
```python
import functools
import math

import jax
import jax.numpy as jnp
from jax import lax
from jax.experimental import pallas as pl
from jax.experimental.pallas import tpu as pltpu
from jax.sharding import Mesh
from jax.sharding import PartitionSpec as P

LAT = ("lat_0", "lat_1", "lat_2", "lat_3")
AXES = ("feat", *LAT)
BF16, F32 = jnp.bfloat16, jnp.float32
TILE = 16
SKEW = 5
SCATTER_AT, PAIR_AT = 3, 12
RESID_AT, COLLECT_BEFORE = 5, 2


def chain_kernel(
    sizes, scale, a_ref, w_hbm, eb_ref, db_ref, gw_ref, geb_ref, gdb_ref,
    w_ref, raw, xs, prod, sig, lats, grads, res, sr, ss, tl, ts, sr2, ss2, tl2, ts2,
    half_out, half_in, half_own, part_out, part_in, pair_out, pair_in, acc, gacc, gebuf,
    w_sem, h_sem, half_sem, xy_sem, core_sem, line_sem, line2_sem, geb_send, geb_recv,
):
    nf, ny, _, nx, _ = sizes
    nq = ny * nx
    nt, per = 2 * nq, nq // 2
    last = nf - 1
    width, nlat = w_ref.shape[1], w_ref.shape[2]
    f, y, h, x, c = (lax.axis_index(name) for name in AXES)
    q = y * nx + x
    mid = last // 2
    lag = SKEW * jnp.maximum(f, last - f)
    partner, sibling = (f, y, 1 - h, x, c), (f, y, h, x, 1 - c)
    after, before = (jnp.minimum(f + 1, last), y, h, x, c), (jnp.maximum(f - 1, 0), y, h, x, c)
    offsets = [(dy, dx) for dy in range(ny) for dx in range(nx) if dy or dx]
    sent = []

    def at_offset(dy, dx):
        return lax.rem(y + dy + ny, ny), lax.rem(x + dx + nx, nx)

    def remote(src, dst, send, recv, to):
        return pltpu.make_async_remote_copy(
            src_ref=src, dst_ref=dst, send_sem=send, recv_sem=recv,
            device_id=to, device_id_type=pl.DeviceIdType.MESH,
        )

    def start(*args):
        copy = remote(*args)
        copy.start()
        sent.append(copy)
        return copy

    w_copy = pltpu.make_async_copy(w_hbm, w_ref, w_sem)
    w_copy.start()

    barrier = pltpu.get_barrier_semaphore()

    def greet(to):
        pl.semaphore_signal(barrier, inc=1, device_id=to, device_id_type=pl.DeviceIdType.MESH)

    greet(partner)
    for dy, dx in offsets:
        py, px = at_offset(dy, dx)
        greet((f, py, h, px, c))
    greet(sibling)

    @pl.when(f > 0)
    def _():
        greet(before)

    @pl.when(f < last)
    def _():
        greet(after)

    @pl.when(f != mid)
    def _():
        greet((mid, y, h, x, c))

    @pl.when(f == 0)
    def _():
        sr[...] = jnp.zeros_like(sr)
        sr2[...] = jnp.zeros_like(sr2)

    @pl.when(f == last)
    def _():
        tl[...] = jnp.zeros_like(tl)
        tl2[...] = jnp.zeros_like(tl2)

    raw[h, c, q] = a_ref[...]
    gacc[...] = jnp.zeros_like(gacc)

    beside = (f > 0).astype(jnp.int32) + (f < last).astype(jnp.int32)
    listeners = last * (f == mid).astype(jnp.int32)
    pl.semaphore_wait(barrier, 2 + len(offsets) + beside + listeners)

    def spread(src, slot, at):
        for number, (dy, dx) in enumerate(offsets):
            py, px = at_offset(dy, dx)
            start(src, slot(c, q), xy_sem.at[0, at, number], xy_sem.at[1, at, q], (f, py, h, px, c))
        start(src, slot(c, q), core_sem.at[0, at, q], core_sem.at[1, at, q], sibling)

    def collect(slot, at):
        for dy, dx in offsets:
            py, px = at_offset(-dy, -dx)
            source = py * nx + px
            here = slot(c, source)
            remote(here, here, xy_sem.at[0, at, 0], xy_sem.at[1, at, source], sibling).wait_recv()
            start(here, here, core_sem.at[0, at, source], core_sem.at[1, at, source], sibling)

    def settle(slot, at):
        for source in range(nq):
            here = slot(1 - c, source)
            remote(here, here, core_sem.at[0, at, 0], core_sem.at[1, at, source], sibling).wait_recv()

    def products(left, tile, count):
        columns = 256
        tiles = pl.ds(tile, count)

        @pl.loop(0, nlat // columns)
        def _(block):
            cols = pl.ds(pl.multiple_of(block * columns, columns), columns)
            total = jnp.dot(
                left[0, tiles].reshape(count * TILE, width), w_ref[0, :, cols], preferred_element_type=F32
            )
            total = total + jnp.dot(
                left[1, tiles].reshape(count * TILE, width), w_ref[1, :, cols], preferred_element_type=F32
            )
            prod[tiles, :, cols] = total.reshape(count, TILE, columns)

    def chain(bufs, sems, order, on_total):
        right_in, right_out, left_in, left_out = bufs

        def to_right(k):
            return remote(right_out.at[k], right_in.at[k], sems.at[0, k], sems.at[1, k], after)

        def to_left(k):
            return remote(left_out.at[k], left_in.at[k], sems.at[2, k], sems.at[3, k], before)

        def steps(low, high, on_step=None):
            @pl.loop(low, high)
            def _(step):
                right, left, done = step - SKEW * f, step - SKEW * (last - f), step - lag

                @pl.when((right >= 0) & (right < nt))
                def _():
                    k = order(right)

                    @pl.when(f > 0)
                    def _():
                        to_right(k).wait_recv()

                    @pl.when(f < last)
                    def _():
                        right_out[k] = (prod[k] + right_in[k].astype(F32)).astype(BF16)
                        to_right(k).start()

                @pl.when((left >= 0) & (left < nt))
                def _():
                    k = order(left)

                    @pl.when(f < last)
                    def _():
                        to_left(k).wait_recv()

                    @pl.when(f > 0)
                    def _():
                        left_out[k] = (prod[k] + left_in[k].astype(F32)).astype(BF16)
                        to_left(k).start()

                @pl.when((done >= 0) & (done < nt))
                def _():
                    k = order(done)
                    on_total(k, prod[k] + right_in[k].astype(F32) + left_in[k].astype(F32))

                if on_step is not None:
                    on_step(step)

        def drain():
            @pl.loop(0, nt)
            def _(k):
                @pl.when(f < last)
                def _():
                    to_right(k).wait_send()

                @pl.when(f > 0)
                def _():
                    to_left(k).wait_send()

        return steps, drain

    far = 1 - h

    def raw_slot(side):
        return lambda core, source: raw.at[side, core, source]

    def unpack(side):
        rows = TILE // 2

        @pl.loop(0, nq)
        def _(source):
            first, second = raw[side, 0, source].astype(F32), raw[side, 1, source].astype(F32)
            tile = (source // per) * nq + side * per + lax.rem(source, per)
            for m in range(2):
                part = slice(m * rows, (m + 1) * rows)
                xs[m, tile] = jnp.concatenate([first[part], second[part]], axis=0).astype(BF16)

    spread(a_ref, raw_slot(h), 0)
    far_copy = start(a_ref, raw.at[h, c, q], h_sem.at[0, 0], h_sem.at[1, 0], partner)
    collect(raw_slot(h), 0)
    far_here = raw.at[far, c, q]
    remote(far_here, far_here, h_sem.at[0, 0], h_sem.at[1, 0], partner).wait_recv()
    spread(far_here, raw_slot(far), 1)
    settle(raw_slot(h), 0)
    unpack(h)
    w_copy.wait()
    products(xs, h * per, per)

    def activate(k, total):
        pre = total + eb_ref[...]
        fall = jnp.exp(-jnp.abs(pre))
        lats[k] = (jnp.maximum(pre, 0.0) + jnp.log1p(fall)).astype(BF16)
        sig[k] = jnp.where(pre >= 0, 1.0, fall) / (1.0 + fall)

    def own_first(k):
        side = lax.rem(k // per + h, 2)
        return (k // nq) * nq + side * per + lax.rem(k, per)

    steps, drain = chain((sr, ss, tl, ts), line_sem, own_first, activate)
    steps(0, per - 1)
    collect(raw_slot(far), 1)
    steps(per - 1, per)
    settle(raw_slot(far), 1)
    unpack(far)
    products(xs, far * per, per)
    steps(per, per + per // 2)
    products(xs, nq, nq)

    def terms(tile, m):
        return lax.dot_general(
            lats[pl.ds(tile, per)].reshape(per * TILE, nlat), w_ref[m],
            (((1,), (1,)), ((), ())), preferred_element_type=F32,
        ).reshape(per, TILE, width)

    def recon(g):
        for m in range(2):
            half_out[g, m] = terms(g * nq + (1 - c) * per, m).astype(BF16)
        start(half_out.at[g], half_in.at[g], half_sem.at[0, g], half_sem.at[1, g], sibling)
        for m in range(2):
            half_own[g, m] = terms(g * nq + c * per, m)

    def own_part(g, owner):
        m, tile = lax.rem(owner, 2), owner // 2
        return half_own[g, m, tile] + half_in[g, m, tile].astype(F32)

    def scatter(g):
        remote(
            half_out.at[g], half_in.at[g], half_sem.at[0, g], half_sem.at[1, g], sibling
        ).wait_recv()
        for number, (dy, dx) in enumerate(offsets):
            py, px = at_offset(dy, dx)
            part_out[g, number] = own_part(g, py * nx + px).astype(BF16)
            start(
                part_out.at[g, number], part_in.at[g, number],
                xy_sem.at[0, 4 + g, number], xy_sem.at[1, 4 + g, number], (f, py, h, px, c),
            )

    def pair_up(g):
        total = own_part(g, q)
        for number in range(len(offsets)):
            here = part_in.at[g, number]
            remote(here, here, xy_sem.at[0, 4 + g, number], xy_sem.at[1, 4 + g, number], sibling).wait_recv()
            total = total + part_in[g, number].astype(F32)
        pair_out[g] = total.astype(BF16)
        start(pair_out.at[g], pair_in.at[g], h_sem.at[0, 1 + g], h_sem.at[1, 1 + g], partner)

    def res_slot(g):
        return lambda core, source: res.at[lax.rem(source, 2), g * nq + core * per + source // 2]

    def residual(g):
        here = pair_in.at[g]
        remote(here, here, h_sem.at[0, 1 + g], h_sem.at[1, 1 + g], partner).wait_recv()
        m, tile = lax.rem(q, 2), g * nq + c * per + q // 2
        bias = jnp.where(m == 0, db_ref[0:1], db_ref[1:2])
        summed = pair_out[g].astype(F32) + pair_in[g].astype(F32)
        res[m, tile] = (scale * summed + bias - xs[m, tile].astype(F32)).astype(BF16)
        spread(res_slot(g)(c, q), res_slot(g), 2 + g)

    ready = nq + lag
    steps(per + per // 2, ready, None)
    recon(0)
    steps(ready, ready + SCATTER_AT)
    scatter(0)
    steps(ready + SCATTER_AT, ready + PAIR_AT)
    pair_up(0)
    steps(ready + PAIR_AT, nt + lag)
    recon(1)
    scatter(1)
    residual(0)
    pair_up(1)
    collect(res_slot(0), 2)
    settle(res_slot(0), 2)
    products(res, 0, nq)

    channels, columns = 128, 256
    across, along = nlat // columns, width // channels
    blocks = 2 * across * along

    def blocks_of(number):
        chan = pl.ds(pl.multiple_of(lax.rem(number // across, along) * channels, channels), channels)
        cols = pl.ds(pl.multiple_of(lax.rem(number, across) * columns, columns), columns)
        return number // (across * along), chan, cols

    def over_rows(left, m, chan, right, cols, low, count):
        tiles = pl.ds(low, count)
        return lax.dot_general(
            left[m, tiles, :, chan].reshape(count * TILE, channels),
            right[tiles, :, cols].reshape(count * TILE, columns),
            (((0,), (0,)), ((), ())), preferred_element_type=F32,
        )

    def dec_block(number):
        m, chan, cols = blocks_of(number)
        acc[m, chan, cols] = scale * over_rows(res, m, chan, lats, cols, 0, nt)

    def enc_block(number):
        m, chan, cols = blocks_of(number)
        acc[m, chan, cols] += over_rows(xs, m, chan, grads, cols, 0, nq)

    def two_a_step(low, block):
        def on_step(step):
            for number in (2 * (step - low), 2 * (step - low) + 1):
                @pl.when(number < blocks)
                def _():
                    block(number)

        return on_step

    def rest(count, block):
        @pl.loop(jnp.minimum(2 * count, blocks), blocks)
        def _(number):
            block(number)

    def finish(k, total):
        grad = scale * total * sig[k]
        grads[k] = grad.astype(BF16)
        gacc[...] += grad

    steps, drain2 = chain((sr2, ss2, tl2, ts2), line2_sem, lambda k: k, finish)
    steps(0, RESID_AT)
    residual(1)
    steps(RESID_AT, nq - COLLECT_BEFORE)
    collect(res_slot(1), 3)
    steps(nq - COLLECT_BEFORE, nq)
    settle(res_slot(1), 3)
    products(res, nq, nq)
    steps(nq, ready, two_a_step(nq, dec_block))
    rest(lag, dec_block)
    steps(ready, nt + lag, two_a_step(ready, enc_block))
    rest(nq, enc_block)

    def to_chip(ahead):
        return remote(
            gebuf, gebuf, geb_send.at[ahead], geb_recv.at[0], (lax.rem(mid + ahead, nf), y, h, x, c)
        )

    @pl.when(f == mid)
    def _():
        gebuf[...] = jnp.broadcast_to(jnp.sum(gacc[...], axis=0, keepdims=True), gebuf.shape)
        for ahead in range(1, nf):
            to_chip(ahead).start()

    @pl.loop(0, blocks)
    def _(number):
        m, chan, cols = blocks_of(number)
        gw_ref[m, chan, cols] = (acc[m, chan, cols] + over_rows(xs, m, chan, grads, cols, nq, nq)).astype(BF16)

    for m in range(2):
        gdb_ref[m : m + 1] = jnp.sum(jnp.sum(res[m].astype(F32), axis=0), axis=0, keepdims=True)

    drain()
    drain2()
    for copy in sent:
        copy.wait_send()

    @pl.when(f == mid)
    def _():
        for ahead in range(1, nf):
            to_chip(ahead).wait_send()

    @pl.when(f != mid)
    def _():
        to_chip(1).wait_recv()

    geb_ref[...] = gebuf[0:1]


def on_device(sizes, acts, weight, enc_bias, dec_bias):
    nf, ny, nh, nx, nc = sizes
    lat_count = ny * nh * nx * nc
    _, width, nlat = weight.shape
    scale = math.sqrt(2.0 * (width * nf) / (nlat * lat_count))
    nq = ny * nx
    nt, per = 2 * nq, nq // 2
    vmem = pltpu.VMEM
    tiles = vmem((2, nt, TILE, width), BF16)
    chunk = vmem((nt, TILE, nlat), BF16)
    wide = vmem((nt, TILE, nlat), F32)
    half = vmem((2, 2, per, TILE, width), BF16)
    pair = vmem((2, TILE, width), BF16)
    parts = vmem((2, nq - 1, TILE, width), BF16)
    dma = pltpu.SemaphoreType.DMA
    whole = pl.BlockSpec(memory_space=pltpu.VMEM)
    grad_weight, grad_enc, grad_dec = pl.pallas_call(
        functools.partial(chain_kernel, sizes, scale),
        out_shape=(
            jax.ShapeDtypeStruct((2, width, nlat), BF16),
            jax.ShapeDtypeStruct((1, nlat), F32),
            jax.ShapeDtypeStruct((2, width), F32),
        ),
        in_specs=[whole, pl.BlockSpec(memory_space=pl.ANY), whole, whole],
        out_specs=(whole, whole, whole),
        scratch_shapes=[
            vmem((2, width, nlat), BF16), vmem((2, 2, nq, TILE, width), BF16),
            tiles, wide, wide, chunk, chunk, tiles,
            *([chunk] * 8),
            half, half, vmem((2, 2, per, TILE, width), F32), parts, parts, pair, pair,
            vmem((2, width, nlat), F32), vmem((TILE, nlat), F32), vmem((8, nlat), F32),
            dma, dma((2, 3)), dma((2, 2)), dma((2, 6, nq)), dma((2, 4, nq)), dma((4, nt)), dma((4, nt)),
            dma((nf,)), dma((1,)),
        ],
        compiler_params=pltpu.CompilerParams(
            collective_id=0, has_side_effects=True, vmem_limit_bytes=60 * 1024 * 1024
        ),
        name="crosscoder_step",
    )(acts.reshape(TILE, width), weight, enc_bias.reshape(1, nlat), dec_bias)
    return grad_weight, grad_enc.reshape(nlat), grad_dec


def solution(mesh):
    shape = dict(mesh.shape)
    if shape["lat"] == 64:
        sizes = (shape["feat"], 4, 2, 4, 2)
    else:
        sizes = (shape["feat"], 1, 2, shape["lat"] // 4, 2)
    torus = Mesh(mesh.devices.reshape(sizes), AXES)
    in_specs = (P(None, LAT, "feat"), P(None, "feat", LAT), P(LAT), P(None, "feat"))
    out_specs = (P(None, "feat", LAT), P(LAT), P(None, "feat"))
    return jax.shard_map(
        functools.partial(on_device, sizes),
        mesh=torus, in_specs=in_specs, out_specs=out_specs, check_vma=False,
    )
```

time: 180 us -> 151 us (0.84)
  Pallas kernels: 172 us -> 146 us
  local copies, waits for them, and re-layouts: 6.23 us -> 4.28 us
    pallas_call x1, Pallas kernels: 172 us -> 146 us  [on_device(): pl.pallas_call(functools.partial(chain_kernel, sizes, scale), out_shape=(...]
    unnamed x5 -> x7, local copies, waits for them, and re-layouts: 4.95 us -> 4.28 us
where the time goes in v2:
time: 151 us
  Pallas kernels  146 us (97%)
  local copies, waits for them, and re-layouts  4.28 us (3%)
    pallas_call x1, Pallas kernels, on_device(): pl.pallas_call(functools.partial(chain_kernel, sizes, scale), out_shape=(...  146 us
    unnamed x7, local copies, waits for them, and re-layouts  4.28 us

profile of v2, /device:TPU:1, one launch (start us, length us, event | category | flops | bytes accessed | tf_op | source)
XLA Modules:
  0.0 151.3 jit_solution(11426012652174567956)
XLA Ops:
  0.6 146.3 %crosscoder_step.1 = (bf16[2,512,1024]{2,1,0:T(8,128)(2,1)}, f32[1,1024]{1,0:T(1,128)}, f32[2,512]{1,0:T(2,128)}) custom-call(bf16[16,512]{1,0:T(8,128)(2,1)} %bitcast.3, bf16[2,512,1024]{2,1,0:T(8,128)(2,1)} %w_hbm.1, f32[1,1024]{1,0:T(1,128)} %bitcast.4, f32[2,512]{1,0:T(2,128)} %db_ref.1), custom_call_target="tpu_custom_call" | custom-call | tf_op jit(solution)/shard_map/crosscoder_step/pallas_call | solution.py:416
  147.0 0.0 copy-start.1
  147.0 0.0 copy-start
  147.0 3.1 %copy.10 = bf16[2,512,1024]{2,1,0:T(8,128)(2,1)} copy(bf16[2,512,1024]{2,1,0:T(8,128)(2,1)} %get-tuple-element.12) | data formatting | bytes 4194304
  150.1 0.0 copy-done.1
  150.1 0.6 copy.11
  150.7 0.0 copy-done
  150.7 0.6 copy.12
Async XLA Ops:
  147.0 3.1 %copy-start.1 = (f32[1,1024]{1,0:T(1,128)S(1)}, f32[1,1024]{1,0:T(1,128)}, u32[]{:S(2)}) copy-start(f32[1,1024]{1,0:T(1,128)} %get-tuple-element.7) | copy-start | bytes 12292
  147.0 3.7 %copy-start = (f32[2,512]{1,0:T(2,128)S(1)}, f32[2,512]{1,0:T(2,128)}, u32[]{:S(2)}) copy-start(f32[2,512]{1,0:T(2,128)} %get-tuple-element.14) | copy-start | bytes 12292

commit v3 on v2

--- a/solution.py
+++ b/solution.py
@@ -13,14 +13,14 @@
 AXES = ("feat", *LAT)
 BF16, F32 = jnp.bfloat16, jnp.float32
 TILE = 16
-SKEW = 5
-SCATTER_AT, PAIR_AT = 3, 12
-RESID_AT, COLLECT_BEFORE = 5, 2
+SKEW = 9
+SCATTER_AT, PAIR_AT = 5, 20
+RESID_AT, COLLECT_BEFORE = 10, 4
 
 
 def chain_kernel(
     sizes, scale, a_ref, w_hbm, eb_ref, db_ref, gw_ref, geb_ref, gdb_ref,
-    w_ref, raw, xs, prod, sig, lats, grads, res, sr, ss, tl, ts, sr2, ss2, tl2, ts2,
+    w_ref, wt, raw, xs, xt, rt, prod, sig, lats, grads, res, sr, ss, tl, ts, sr2, ss2, tl2, ts2,
     half_out, half_in, half_own, part_out, part_in, pair_out, pair_in, acc, gacc, gebuf,
     w_sem, h_sem, half_sem, xy_sem, core_sem, line_sem, line2_sem, geb_send, geb_recv,
 ):
@@ -116,19 +116,20 @@
             remote(here, here, core_sem.at[0, at, 0], core_sem.at[1, at, source], sibling).wait_recv()
 
     def products(left, tile, count):
-        columns = 256
         tiles = pl.ds(tile, count)
-
-        @pl.loop(0, nlat // columns)
-        def _(block):
-            cols = pl.ds(pl.multiple_of(block * columns, columns), columns)
-            total = jnp.dot(
-                left[0, tiles].reshape(count * TILE, width), w_ref[0, :, cols], preferred_element_type=F32
-            )
-            total = total + jnp.dot(
-                left[1, tiles].reshape(count * TILE, width), w_ref[1, :, cols], preferred_element_type=F32
-            )
-            prod[tiles, :, cols] = total.reshape(count, TILE, columns)
+        total = jnp.dot(left[0, tiles].reshape(count * TILE, width), w_ref[0], preferred_element_type=F32)
+        total = total + jnp.dot(left[1, tiles].reshape(count * TILE, width), w_ref[1], preferred_element_type=F32)
+        prod[tiles] = total.reshape(count, TILE, nlat)
+
+    def turned(left, right):
+        for m in range(2):
+            right[m] = left[m].reshape(nt * TILE, width).T
+
+    piece = nlat // 2
+    pieces = 2 * nt
+
+    def half_of(k):
+        return pl.ds(pl.multiple_of(lax.rem(k, 2) * piece, piece), piece)
 
     def chain(bufs, sems, order, on_total):
         right_in, right_out, left_in, left_out = bufs
@@ -144,9 +145,9 @@
             def _(step):
                 right, left, done = step - SKEW * f, step - SKEW * (last - f), step - lag
 
-                @pl.when((right >= 0) & (right < nt))
+                @pl.when((right >= 0) & (right < pieces))
                 def _():
-                    k = order(right)
+                    tile, k, cols = order(right)
 
                     @pl.when(f > 0)
                     def _():
@@ -154,12 +155,12 @@
 
                     @pl.when(f < last)
                     def _():
-                        right_out[k] = (prod[k] + right_in[k].astype(F32)).astype(BF16)
+                        right_out[k] = (prod[tile, :, cols] + right_in[k].astype(F32)).astype(BF16)
                         to_right(k).start()
 
-                @pl.when((left >= 0) & (left < nt))
+                @pl.when((left >= 0) & (left < pieces))
                 def _():
-                    k = order(left)
+                    tile, k, cols = order(left)
 
                     @pl.when(f < last)
                     def _():
@@ -167,19 +168,19 @@
 
                     @pl.when(f > 0)
                     def _():
-                        left_out[k] = (prod[k] + left_in[k].astype(F32)).astype(BF16)
+                        left_out[k] = (prod[tile, :, cols] + left_in[k].astype(F32)).astype(BF16)
                         to_left(k).start()
 
-                @pl.when((done >= 0) & (done < nt))
+                @pl.when((done >= 0) & (done < pieces))
                 def _():
-                    k = order(done)
-                    on_total(k, prod[k] + right_in[k].astype(F32) + left_in[k].astype(F32))
+                    tile, k, cols = order(done)
+                    on_total(tile, cols, prod[tile, :, cols] + right_in[k].astype(F32) + left_in[k].astype(F32))
 
                 if on_step is not None:
                     on_step(step)
 
         def drain():
-            @pl.loop(0, nt)
+            @pl.loop(0, pieces)
             def _(k):
                 @pl.when(f < last)
                 def _():
@@ -207,41 +208,45 @@
                 part = slice(m * rows, (m + 1) * rows)
                 xs[m, tile] = jnp.concatenate([first[part], second[part]], axis=0).astype(BF16)
 
+    start(a_ref, raw.at[h, c, q], h_sem.at[0, 0], h_sem.at[1, 0], partner)
     spread(a_ref, raw_slot(h), 0)
-    far_copy = start(a_ref, raw.at[h, c, q], h_sem.at[0, 0], h_sem.at[1, 0], partner)
+    w_copy.wait()
+    for m in range(2):
+        wt[m] = w_ref[m].T
     collect(raw_slot(h), 0)
     far_here = raw.at[far, c, q]
     remote(far_here, far_here, h_sem.at[0, 0], h_sem.at[1, 0], partner).wait_recv()
     spread(far_here, raw_slot(far), 1)
     settle(raw_slot(h), 0)
     unpack(h)
-    w_copy.wait()
     products(xs, h * per, per)
 
-    def activate(k, total):
-        pre = total + eb_ref[...]
+    def activate(k, cols, total):
+        pre = total + eb_ref[:, cols]
         fall = jnp.exp(-jnp.abs(pre))
-        lats[k] = (jnp.maximum(pre, 0.0) + jnp.log1p(fall)).astype(BF16)
-        sig[k] = jnp.where(pre >= 0, 1.0, fall) / (1.0 + fall)
-
-    def own_first(k):
+        lats[k, :, cols] = (jnp.maximum(pre, 0.0) + jnp.log1p(fall)).astype(BF16)
+        sig[k, :, cols] = jnp.where(pre >= 0, 1.0, fall) / (1.0 + fall)
+
+    def own_first(number):
+        k = number // 2
         side = lax.rem(k // per + h, 2)
-        return (k // nq) * nq + side * per + lax.rem(k, per)
+        tile = (k // nq) * nq + side * per + lax.rem(k, per)
+        return tile, 2 * tile + lax.rem(number, 2), half_of(number)
 
     steps, drain = chain((sr, ss, tl, ts), line_sem, own_first, activate)
-    steps(0, per - 1)
+    steps(0, nq - 2)
     collect(raw_slot(far), 1)
-    steps(per - 1, per)
+    steps(nq - 2, nq)
     settle(raw_slot(far), 1)
     unpack(far)
     products(xs, far * per, per)
-    steps(per, per + per // 2)
+    steps(nq, nq + per)
     products(xs, nq, nq)
 
     def terms(tile, m):
         return lax.dot_general(
-            lats[pl.ds(tile, per)].reshape(per * TILE, nlat), w_ref[m],
-            (((1,), (1,)), ((), ())), preferred_element_type=F32,
+            lats[pl.ds(tile, per)].reshape(per * TILE, nlat), wt[m],
+            (((1,), (0,)), ((), ())), preferred_element_type=F32,
         ).reshape(per, TILE, width)
 
     def recon(g):
@@ -288,78 +293,65 @@
         res[m, tile] = (scale * summed + bias - xs[m, tile].astype(F32)).astype(BF16)
         spread(res_slot(g)(c, q), res_slot(g), 2 + g)
 
-    ready = nq + lag
-    steps(per + per // 2, ready, None)
+    ready = nt + lag
+    steps(nq + per, ready)
     recon(0)
     steps(ready, ready + SCATTER_AT)
     scatter(0)
     steps(ready + SCATTER_AT, ready + PAIR_AT)
     pair_up(0)
-    steps(ready + PAIR_AT, nt + lag)
+    steps(ready + PAIR_AT, pieces + lag)
     recon(1)
     scatter(1)
     residual(0)
+    turned(xs, xt)
     pair_up(1)
     collect(res_slot(0), 2)
     settle(res_slot(0), 2)
     products(res, 0, nq)
 
-    channels, columns = 128, 256
-    across, along = nlat // columns, width // channels
-    blocks = 2 * across * along
-
-    def blocks_of(number):
-        chan = pl.ds(pl.multiple_of(lax.rem(number // across, along) * channels, channels), channels)
-        cols = pl.ds(pl.multiple_of(lax.rem(number, across) * columns, columns), columns)
-        return number // (across * along), chan, cols
-
-    def over_rows(left, m, chan, right, cols, low, count):
-        tiles = pl.ds(low, count)
-        return lax.dot_general(
-            left[m, tiles, :, chan].reshape(count * TILE, channels),
-            right[tiles, :, cols].reshape(count * TILE, columns),
-            (((0,), (0,)), ((), ())), preferred_element_type=F32,
+    below = nq * TILE
+
+    def dec_block(number):
+        m, cols = number // 2, half_of(number)
+        acc[m, :, cols] = scale * jnp.dot(
+            rt[m], lats[:, :, cols].reshape(nt * TILE, piece), preferred_element_type=F32
         )
 
-    def dec_block(number):
-        m, chan, cols = blocks_of(number)
-        acc[m, chan, cols] = scale * over_rows(res, m, chan, lats, cols, 0, nt)
-
     def enc_block(number):
-        m, chan, cols = blocks_of(number)
-        acc[m, chan, cols] += over_rows(xs, m, chan, grads, cols, 0, nq)
-
-    def two_a_step(low, block):
+        m, cols = number // 2, half_of(number)
+        acc[m, :, cols] += jnp.dot(
+            xt[m, :, :below], grads[:nq, :, cols].reshape(below, piece), preferred_element_type=F32
+        )
+
+    def blocks_from(low, block):
         def on_step(step):
-            for number in (2 * (step - low), 2 * (step - low) + 1):
-                @pl.when(number < blocks)
-                def _():
-                    block(number)
+            @pl.when(step - low < 4)
+            def _():
+                block(step - low)
 
         return on_step
 
-    def rest(count, block):
-        @pl.loop(jnp.minimum(2 * count, blocks), blocks)
-        def _(number):
-            block(number)
-
-    def finish(k, total):
-        grad = scale * total * sig[k]
-        grads[k] = grad.astype(BF16)
-        gacc[...] += grad
-
-    steps, drain2 = chain((sr2, ss2, tl2, ts2), line2_sem, lambda k: k, finish)
+    def finish(k, cols, total):
+        grad = scale * total * sig[k, :, cols]
+        grads[k, :, cols] = grad.astype(BF16)
+        gacc[:, cols] += grad
+
+    steps, drain2 = chain(
+        (sr2, ss2, tl2, ts2), line2_sem, lambda number: (number // 2, number, half_of(number)), finish
+    )
     steps(0, RESID_AT)
     residual(1)
-    steps(RESID_AT, nq - COLLECT_BEFORE)
+    steps(RESID_AT, nt - COLLECT_BEFORE)
     collect(res_slot(1), 3)
-    steps(nq - COLLECT_BEFORE, nq)
+    steps(nt - COLLECT_BEFORE, nt)
     settle(res_slot(1), 3)
     products(res, nq, nq)
-    steps(nq, ready, two_a_step(nq, dec_block))
-    rest(lag, dec_block)
-    steps(ready, nt + lag, two_a_step(ready, enc_block))
-    rest(nq, enc_block)
+    turned(res, rt)
+    for m in range(2):
+        gdb_ref[m : m + 1] = jnp.sum(jnp.sum(res[m].astype(F32), axis=0), axis=0, keepdims=True)
+    steps(nt, ready, blocks_from(nt, dec_block))
+    steps(ready, pieces + lag, blocks_from(ready, enc_block))
 
     def to_chip(ahead):
         return remote(
@@ -372,13 +364,9 @@
         for ahead in range(1, nf):
             to_chip(ahead).start()
 
-    @pl.loop(0, blocks)
-    def _(number):
-        m, chan, cols = blocks_of(number)
-        gw_ref[m, chan, cols] = (acc[m, chan, cols] + over_rows(xs, m, chan, grads, cols, nq, nq)).astype(BF16)
-
     for m in range(2):
-        gdb_ref[m : m + 1] = jnp.sum(jnp.sum(res[m].astype(F32), axis=0), axis=0, keepdims=True)
+        rest = jnp.dot(xt[m, :, below:], grads[nq:].reshape(below, nlat), preferred_element_type=F32)
+        gw_ref[m] = (acc[m] + rest).astype(BF16)
 
     drain()
     drain2()
@@ -408,6 +396,8 @@
     tiles = vmem((2, nt, TILE, width), BF16)
     chunk = vmem((nt, TILE, nlat), BF16)
     wide = vmem((nt, TILE, nlat), F32)
+    flow = vmem((2 * nt, TILE, nlat // 2), BF16)
+    turned = vmem((2, width, nt * TILE), BF16)
     half = vmem((2, 2, per, TILE, width), BF16)
     pair = vmem((2, TILE, width), BF16)
     parts = vmem((2, nq - 1, TILE, width), BF16)
@@ -423,12 +413,12 @@
         in_specs=[whole, pl.BlockSpec(memory_space=pl.ANY), whole, whole],
         out_specs=(whole, whole, whole),
         scratch_shapes=[
-            vmem((2, width, nlat), BF16), vmem((2, 2, nq, TILE, width), BF16),
-            tiles, wide, wide, chunk, chunk, tiles,
-            *([chunk] * 8),
+            vmem((2, width, nlat), BF16), vmem((2, nlat, width), BF16), vmem((2, 2, nq, TILE, width), BF16),
+            tiles, turned, turned, wide, wide, chunk, chunk, tiles,
+            *([flow] * 8),
             half, half, vmem((2, 2, per, TILE, width), F32), parts, parts, pair, pair,
             vmem((2, width, nlat), F32), vmem((TILE, nlat), F32), vmem((8, nlat), F32),
-            dma, dma((2, 3)), dma((2, 2)), dma((2, 6, nq)), dma((2, 4, nq)), dma((4, nt)), dma((4, nt)),
+            dma, dma((2, 3)), dma((2, 2)), dma((2, 6, nq)), dma((2, 4, nq)), dma((4, 2 * nt)), dma((4, 2 * nt)),
             dma((nf,)), dma((1,)),
         ],
         compiler_params=pltpu.CompilerParams(

time: 151 us -> 142 us (0.940)
  Pallas kernels: 146 us -> 137 us
    pallas_call x1, Pallas kernels: 146 us -> 137 us  [on_device(): pl.pallas_call(functools.partial(chain_kernel, sizes, scale), out_shape=(...]
where the time goes in v3:
time: 142 us
  Pallas kernels  137 us (96%)
  local copies, waits for them, and re-layouts  4.28 us (3%)
    pallas_call x1, Pallas kernels, on_device(): pl.pallas_call(functools.partial(chain_kernel, sizes, scale), out_shape=(...  137 us
    unnamed x7, local copies, waits for them, and re-layouts  4.28 us

profile of v3, /device:TPU:1, one launch (start us, length us, event | category | flops | bytes accessed | tf_op | source)
XLA Modules:
  0.0 141.7 jit_solution(3983017258075014165)
XLA Ops:
  0.6 136.8 %crosscoder_step.1 = (bf16[2,512,1024]{2,1,0:T(8,128)(2,1)}, f32[1,1024]{1,0:T(1,128)}, f32[2,512]{1,0:T(2,128)}) custom-call(bf16[16,512]{1,0:T(8,128)(2,1)} %bitcast.3, bf16[2,512,1024]{2,1,0:T(8,128)(2,1)} %w_hbm.1, f32[1,1024]{1,0:T(1,128)} %bitcast.4, f32[2,512]{1,0:T(2,128)} %db_ref.1), custom_call_target="tpu_custom_call" | custom-call | tf_op jit(solution)/shard_map/crosscoder_step/pallas_call | solution.py:406
  137.5 0.0 copy-start.1
  137.5 0.0 copy-start
  137.5 3.1 %copy.10 = bf16[2,512,1024]{2,1,0:T(8,128)(2,1)} copy(bf16[2,512,1024]{2,1,0:T(8,128)(2,1)} %get-tuple-element.12) | data formatting | bytes 4194304
  140.6 0.0 copy-done.1
  140.6 0.6 copy.11
  141.2 0.0 copy-done
  141.2 0.6 copy.12
Async XLA Ops:
  137.5 3.1 %copy-start.1 = (f32[1,1024]{1,0:T(1,128)S(1)}, f32[1,1024]{1,0:T(1,128)}, u32[]{:S(2)}) copy-start(f32[1,1024]{1,0:T(1,128)} %get-tuple-element.7) | copy-start | bytes 12292
  137.5 3.7 %copy-start = (f32[2,512]{1,0:T(2,128)S(1)}, f32[2,512]{1,0:T(2,128)}, u32[]{:S(2)}) copy-start(f32[2,512]{1,0:T(2,128)} %get-tuple-element.14) | copy-start | bytes 12292

commit v4 on v3

--- a/solution.py
+++ b/solution.py
@@ -14,8 +14,7 @@
 BF16, F32 = jnp.bfloat16, jnp.float32
 TILE = 16
 SKEW = 9
-SCATTER_AT, PAIR_AT = 5, 20
-RESID_AT, COLLECT_BEFORE = 10, 4
+GROUPS = 4
 
 
 def chain_kernel(
@@ -26,7 +25,8 @@
 ):
     nf, ny, _, nx, _ = sizes
     nq = ny * nx
-    nt, per = 2 * nq, nq // 2
+    nt, per = 2 * nq, nq // GROUPS
+    split = GROUPS // 2
     last = nf - 1
     width, nlat = w_ref.shape[1], w_ref.shape[2]
     f, y, h, x, c = (lax.axis_index(name) for name in AXES)
@@ -115,11 +115,16 @@
             here = slot(1 - c, source)
             remote(here, here, core_sem.at[0, at, 0], core_sem.at[1, at, source], sibling).wait_recv()
 
-    def products(left, tile, count):
-        tiles = pl.ds(tile, count)
-        total = jnp.dot(left[0, tiles].reshape(count * TILE, width), w_ref[0], preferred_element_type=F32)
-        total = total + jnp.dot(left[1, tiles].reshape(count * TILE, width), w_ref[1], preferred_element_type=F32)
-        prod[tiles] = total.reshape(count, TILE, nlat)
+    def products(left, count, *tiles):
+        rows = count * TILE
+
+        def of_model(m):
+            parts = [left[m, pl.ds(tile, count)].reshape(rows, width) for tile in tiles]
+            return jnp.dot(jnp.concatenate(parts, axis=0), w_ref[m], preferred_element_type=F32)
+
+        total = of_model(0) + of_model(1)
+        for number, tile in enumerate(tiles):
+            prod[pl.ds(tile, count)] = total[number * rows : (number + 1) * rows].reshape(count, TILE, nlat)
 
     def turned(left, right):
         for m in range(2):
@@ -203,7 +208,7 @@
         @pl.loop(0, nq)
         def _(source):
             first, second = raw[side, 0, source].astype(F32), raw[side, 1, source].astype(F32)
-            tile = (source // per) * nq + side * per + lax.rem(source, per)
+            tile = (source // per) * 2 * per + side * per + lax.rem(source, per)
             for m in range(2):
                 part = slice(m * rows, (m + 1) * rows)
                 xs[m, tile] = jnp.concatenate([first[part], second[part]], axis=0).astype(BF16)
@@ -219,7 +224,7 @@
     spread(far_here, raw_slot(far), 1)
     settle(raw_slot(h), 0)
     unpack(h)
-    products(xs, h * per, per)
+    products(xs, per, h * per, (2 + h) * per)
 
     def activate(k, cols, total):
         pre = total + eb_ref[:, cols]
@@ -229,8 +234,10 @@
 
     def own_first(number):
         k = number // 2
-        side = lax.rem(k // per + h, 2)
-        tile = (k // nq) * nq + side * per + lax.rem(k, per)
+        late, turn = k // (4 * per), lax.rem(k // per, 4)
+        side = jnp.where(late == 0, turn // 2, lax.rem(turn, 2))
+        group = jnp.where(late == 0, lax.rem(turn, 2), turn // 2 + 2 * late)
+        tile = group * 2 * per + lax.rem(side + h, 2) * per + lax.rem(k, per)
         return tile, 2 * tile + lax.rem(number, 2), half_of(number)
 
     steps, drain = chain((sr, ss, tl, ts), line_sem, own_first, activate)
@@ -239,8 +246,8 @@
     steps(nq - 2, nq)
     settle(raw_slot(far), 1)
     unpack(far)
-    products(xs, far * per, per)
-    steps(nq, nq + per)
+    products(xs, per, far * per, (2 + far) * per)
+    steps(nq, nq + nq // 4)
     products(xs, nq, nq)
 
     def terms(tile, m):
@@ -251,14 +258,20 @@
 
     def recon(g):
         for m in range(2):
-            half_out[g, m] = terms(g * nq + (1 - c) * per, m).astype(BF16)
+            half_out[g, m] = terms((2 * g + 1 - c) * per, m).astype(BF16)
         start(half_out.at[g], half_in.at[g], half_sem.at[0, g], half_sem.at[1, g], sibling)
         for m in range(2):
-            half_own[g, m] = terms(g * nq + c * per, m)
+            half_own[g, m] = terms((2 * g + c) * per, m)
+
+    part_width = width // split
+
+    def block_of(owner):
+        first = pl.multiple_of(lax.rem(owner, split) * part_width, part_width)
+        return lax.rem(owner // split, 2), owner // (2 * split), pl.ds(first, part_width)
 
     def own_part(g, owner):
-        m, tile = lax.rem(owner, 2), owner // 2
-        return half_own[g, m, tile] + half_in[g, m, tile].astype(F32)
+        m, tile, chan = block_of(owner)
+        return half_own[g, m, tile, :, chan] + half_in[g, m, tile, :, chan].astype(F32)
 
     def scatter(g):
         remote(
@@ -269,46 +282,63 @@
             part_out[g, number] = own_part(g, py * nx + px).astype(BF16)
             start(
                 part_out.at[g, number], part_in.at[g, number],
-                xy_sem.at[0, 4 + g, number], xy_sem.at[1, 4 + g, number], (f, py, h, px, c),
+                xy_sem.at[0, 2 + GROUPS + g, number], xy_sem.at[1, 2 + GROUPS + g, number], (f, py, h, px, c),
             )
 
     def pair_up(g):
         total = own_part(g, q)
         for number in range(len(offsets)):
             here = part_in.at[g, number]
-            remote(here, here, xy_sem.at[0, 4 + g, number], xy_sem.at[1, 4 + g, number], sibling).wait_recv()
+            remote(here, here, xy_sem.at[0, 2 + GROUPS + g, number], xy_sem.at[1, 2 + GROUPS + g, number], sibling).wait_recv()
             total = total + part_in[g, number].astype(F32)
         pair_out[g] = total.astype(BF16)
         start(pair_out.at[g], pair_in.at[g], h_sem.at[0, 1 + g], h_sem.at[1, 1 + g], partner)
 
     def res_slot(g):
-        return lambda core, source: res.at[lax.rem(source, 2), g * nq + core * per + source // 2]
+        def slot(core, source):
+            m, tile, chan = block_of(source)
+            return res.at[m, (2 * g + core) * per + tile, :, chan]
+
+        return slot
 
     def residual(g):
         here = pair_in.at[g]
         remote(here, here, h_sem.at[0, 1 + g], h_sem.at[1, 1 + g], partner).wait_recv()
-        m, tile = lax.rem(q, 2), g * nq + c * per + q // 2
-        bias = jnp.where(m == 0, db_ref[0:1], db_ref[1:2])
+        m, tile, chan = block_of(q)
+        tile = (2 * g + c) * per + tile
+        bias = jnp.where(m == 0, db_ref[0:1, chan], db_ref[1:2, chan])
         summed = pair_out[g].astype(F32) + pair_in[g].astype(F32)
-        res[m, tile] = (scale * summed + bias - xs[m, tile].astype(F32)).astype(BF16)
+        res[m, tile, :, chan] = (scale * summed + bias - xs[m, tile, :, chan].astype(F32)).astype(BF16)
         spread(res_slot(g)(c, q), res_slot(g), 2 + g)
 
+    def gather(g):
+        collect(res_slot(g), 2 + g)
+
+    def arrived(g):
+        settle(res_slot(g), 2 + g)
+        products(res, 2 * per, 2 * g * per)
+
+    def run(low, base, plan, high):
+        for at, stage, g in plan:
+            steps(low, base + at)
+            stage(g)
+            low = base + at
+        steps(low, high)
+
     ready = nt + lag
-    steps(nq + per, ready)
-    recon(0)
-    steps(ready, ready + SCATTER_AT)
-    scatter(0)
-    steps(ready + SCATTER_AT, ready + PAIR_AT)
-    pair_up(0)
-    steps(ready + PAIR_AT, pieces + lag)
-    recon(1)
-    scatter(1)
-    residual(0)
+    first = 6 * per
+    run(nq + nq // 4, lag, [
+        (first, recon, 0), (first + nq // 4, scatter, 0), (8 * per, recon, 1), (8 * per + nq // 4, scatter, 1),
+        (10 * per + nq // 8, pair_up, 0), (12 * per, recon, 2), (12 * per + nq // 8, pair_up, 1),
+        (13 * per, scatter, 2), (15 * per + nq // 8, residual, 0),
+    ], pieces + lag)
+    recon(3)
+    pair_up(2)
+    scatter(3)
+    residual(1)
     turned(xs, xt)
-    pair_up(1)
-    collect(res_slot(0), 2)
-    settle(res_slot(0), 2)
-    products(res, 0, nq)
+    gather(0)
+    arrived(0)
 
     below = nq * TILE
 
@@ -340,17 +370,15 @@
     steps, drain2 = chain(
         (sr2, ss2, tl2, ts2), line2_sem, lambda number: (number // 2, number, half_of(number)), finish
     )
-    steps(0, RESID_AT)
-    residual(1)
-    steps(RESID_AT, nt - COLLECT_BEFORE)
-    collect(res_slot(1), 3)
-    steps(nt - COLLECT_BEFORE, nt)
-    settle(res_slot(1), 3)
-    products(res, nq, nq)
+    run(0, 0, [
+        (nq // 8, pair_up, 3), (nq // 4 + nq // 8, gather, 1), (nq // 4 + nq // 8, residual, 2), (2 * per, arrived, 1),
+        (5 * per + nq // 8, gather, 2), (5 * per + nq // 8, residual, 3), (6 * per, arrived, 2),
+        (9 * per + nq // 8, gather, 3), (10 * per, arrived, 3),
+    ], 10 * per)
     turned(res, rt)
     for m in range(2):
         gdb_ref[m : m + 1] = jnp.sum(jnp.sum(res[m].astype(F32), axis=0), axis=0, keepdims=True)
-    steps(nt, ready, blocks_from(nt, dec_block))
+    steps(10 * per, ready, blocks_from(10 * per, dec_block))
     steps(ready, pieces + lag, blocks_from(ready, enc_block))
 
     def to_chip(ahead):
@@ -391,16 +419,16 @@
     _, width, nlat = weight.shape
     scale = math.sqrt(2.0 * (width * nf) / (nlat * lat_count))
     nq = ny * nx
-    nt, per = 2 * nq, nq // 2
+    nt, per = 2 * nq, nq // GROUPS
     vmem = pltpu.VMEM
     tiles = vmem((2, nt, TILE, width), BF16)
     chunk = vmem((nt, TILE, nlat), BF16)
     wide = vmem((nt, TILE, nlat), F32)
     flow = vmem((2 * nt, TILE, nlat // 2), BF16)
     turned = vmem((2, width, nt * TILE), BF16)
-    half = vmem((2, 2, per, TILE, width), BF16)
-    pair = vmem((2, TILE, width), BF16)
-    parts = vmem((2, nq - 1, TILE, width), BF16)
+    half = vmem((GROUPS, 2, per, TILE, width), BF16)
+    pair = vmem((GROUPS, TILE, 2 * width // GROUPS), BF16)
+    parts = vmem((GROUPS, nq - 1, TILE, 2 * width // GROUPS), BF16)
     dma = pltpu.SemaphoreType.DMA
     whole = pl.BlockSpec(memory_space=pltpu.VMEM)
     grad_weight, grad_enc, grad_dec = pl.pallas_call(
@@ -416,9 +444,9 @@
             vmem((2, width, nlat), BF16), vmem((2, nlat, width), BF16), vmem((2, 2, nq, TILE, width), BF16),
             tiles, turned, turned, wide, wide, chunk, chunk, tiles,
             *([flow] * 8),
-            half, half, vmem((2, 2, per, TILE, width), F32), parts, parts, pair, pair,
+            half, half, vmem((GROUPS, 2, per, TILE, width), F32), parts, parts, pair, pair,
             vmem((2, width, nlat), F32), vmem((TILE, nlat), F32), vmem((8, nlat), F32),
-            dma, dma((2, 3)), dma((2, 2)), dma((2, 6, nq)), dma((2, 4, nq)), dma((4, 2 * nt)), dma((4, 2 * nt)),
+            dma, dma((2, 1 + GROUPS)), dma((2, GROUPS)), dma((2, 2 + 2 * GROUPS, nq)), dma((2, 2 + GROUPS, nq)), dma((4, 2 * nt)), dma((4, 2 * nt)),
             dma((nf,)), dma((1,)),
         ],
         compiler_params=pltpu.CompilerParams(

time: 142 us -> 141 us (level)
  Pallas kernels: 137 us -> 135 us
where the time goes in v4:
time: 141 us; the launch traced here: 140 us
  Pallas kernels  135 us (96%)
  local copies, waits for them, and re-layouts  4.28 us (3%)
    pallas_call x1, Pallas kernels, on_device(): pl.pallas_call(functools.partial(chain_kernel, sizes, scale), out_shape=(...  135 us
    unnamed x7, local copies, waits for them, and re-layouts  4.28 us

profile of v4, /device:TPU:1, one launch (start us, length us, event | category | flops | bytes accessed | tf_op | source)
XLA Modules:
  0.0 140.4 jit_solution(3726657565709649168)
XLA Ops:
  0.6 135.5 %crosscoder_step.1 = (bf16[2,512,1024]{2,1,0:T(8,128)(2,1)}, f32[1,1024]{1,0:T(1,128)}, f32[2,512]{1,0:T(2,128)}) custom-call(bf16[16,512]{1,0:T(8,128)(2,1)} %bitcast.3, bf16[2,512,1024]{2,1,0:T(8,128)(2,1)} %w_hbm.1, f32[1,1024]{1,0:T(1,128)} %bitcast.4, f32[2,512]{1,0:T(2,128)} %db_ref.1), custom_call_target="tpu_custom_call" | custom-call | tf_op jit(solution)/shard_map/crosscoder_step/pallas_call | solution.py:434
  136.1 0.0 copy-start.1
  136.1 0.0 copy-start
  136.1 3.1 %copy.10 = bf16[2,512,1024]{2,1,0:T(8,128)(2,1)} copy(bf16[2,512,1024]{2,1,0:T(8,128)(2,1)} %get-tuple-element.12) | data formatting | bytes 4194304
  139.2 0.0 copy-done.1
  139.2 0.6 copy.11
  139.8 0.0 copy-done
  139.8 0.6 copy.12
Async XLA Ops:
  136.1 3.1 %copy-start.1 = (f32[1,1024]{1,0:T(1,128)S(1)}, f32[1,1024]{1,0:T(1,128)}, u32[]{:S(2)}) copy-start(f32[1,1024]{1,0:T(1,128)} %get-tuple-element.7) | copy-start | bytes 12292
  136.1 3.7 %copy-start = (f32[2,512]{1,0:T(2,128)S(1)}, f32[2,512]{1,0:T(2,128)}, u32[]{:S(2)}) copy-start(f32[2,512]{1,0:T(2,128)} %get-tuple-element.14) | copy-start | bytes 12292

commit v5 on v4

--- a/solution.py
+++ b/solution.py
@@ -18,10 +18,10 @@
 
 
 def chain_kernel(
-    sizes, scale, a_ref, w_hbm, eb_ref, db_ref, gw_ref, geb_ref, gdb_ref,
+    sizes, scale, a_ref, w_hbm, eb_ref, db_ref, acc_out, xt_out, grads_out, geb_ref, gdb_ref,
     w_ref, wt, raw, xs, xt, rt, prod, sig, lats, grads, res, sr, ss, tl, ts, sr2, ss2, tl2, ts2,
     half_out, half_in, half_own, part_out, part_in, pair_out, pair_in, acc, gacc, gebuf,
-    w_sem, h_sem, half_sem, xy_sem, core_sem, line_sem, line2_sem, geb_send, geb_recv,
+    w_sem, h_sem, half_sem, xy_sem, core_sem, line_sem, line2_sem, geb_send, geb_recv, out_sem,
 ):
     nf, ny, _, nx, _ = sizes
     nq = ny * nx
@@ -379,7 +379,16 @@
     for m in range(2):
         gdb_ref[m : m + 1] = jnp.sum(jnp.sum(res[m].astype(F32), axis=0), axis=0, keepdims=True)
     steps(10 * per, ready, blocks_from(10 * per, dec_block))
-    steps(ready, pieces + lag, blocks_from(ready, enc_block))
+    steps(ready, ready + 4, blocks_from(ready, enc_block))
+    outs = [
+        pltpu.make_async_copy(acc, acc_out, out_sem.at[0]),
+        pltpu.make_async_copy(xt.at[:, :, pl.ds(below, below)], xt_out, out_sem.at[1]),
+        pltpu.make_async_copy(grads.at[pl.ds(nq, nq)], grads_out, out_sem.at[2]),
+    ]
+    outs[0].start()
+    outs[1].start()
+    steps(ready + 4, pieces + lag)
+    outs[2].start()
 
     def to_chip(ahead):
         return remote(
@@ -392,10 +401,6 @@
         for ahead in range(1, nf):
             to_chip(ahead).start()
 
-    for m in range(2):
-        rest = jnp.dot(xt[m, :, below:], grads[nq:].reshape(below, nlat), preferred_element_type=F32)
-        gw_ref[m] = (acc[m] + rest).astype(BF16)
-
     drain()
     drain2()
     for copy in sent:
@@ -411,6 +416,15 @@
         to_chip(1).wait_recv()
 
     geb_ref[...] = gebuf[0:1]
+    for copy in outs:
+        copy.wait()
+
+
+def last_product(acc_ref, xt_ref, grads_ref, geb_in, gdb_in, gw_ref, geb_ref, gdb_ref):
+    rest = jnp.dot(xt_ref[0], grads_ref[...], preferred_element_type=F32)
+    gw_ref[0] = (acc_ref[0] + rest).astype(BF16)
+    geb_ref[...] = geb_in[...]
+    gdb_ref[...] = gdb_in[...]
 
 
 def on_device(sizes, acts, weight, enc_bias, dec_bias):
@@ -431,15 +445,19 @@
     parts = vmem((GROUPS, nq - 1, TILE, 2 * width // GROUPS), BF16)
     dma = pltpu.SemaphoreType.DMA
     whole = pl.BlockSpec(memory_space=pltpu.VMEM)
-    grad_weight, grad_enc, grad_dec = pl.pallas_call(
+    anywhere = pl.BlockSpec(memory_space=pl.ANY)
+    below = nq * TILE
+    acc, xt, grads, geb, gdb = pl.pallas_call(
         functools.partial(chain_kernel, sizes, scale),
         out_shape=(
-            jax.ShapeDtypeStruct((2, width, nlat), BF16),
+            jax.ShapeDtypeStruct((2, width, nlat), F32),
+            jax.ShapeDtypeStruct((2, width, below), BF16),
+            jax.ShapeDtypeStruct((nq, TILE, nlat), BF16),
             jax.ShapeDtypeStruct((1, nlat), F32),
             jax.ShapeDtypeStruct((2, width), F32),
         ),
         in_specs=[whole, pl.BlockSpec(memory_space=pl.ANY), whole, whole],
-        out_specs=(whole, whole, whole),
+        out_specs=(anywhere, anywhere, anywhere, whole, whole),
         scratch_shapes=[
             vmem((2, width, nlat), BF16), vmem((2, nlat, width), BF16), vmem((2, 2, nq, TILE, width), BF16),
             tiles, turned, turned, wide, wide, chunk, chunk, tiles,
@@ -447,13 +465,36 @@
             half, half, vmem((GROUPS, 2, per, TILE, width), F32), parts, parts, pair, pair,
             vmem((2, width, nlat), F32), vmem((TILE, nlat), F32), vmem((8, nlat), F32),
             dma, dma((2, 1 + GROUPS)), dma((2, GROUPS)), dma((2, 2 + 2 * GROUPS, nq)), dma((2, 2 + GROUPS, nq)), dma((4, 2 * nt)), dma((4, 2 * nt)),
-            dma((nf,)), dma((1,)),
+            dma((nf,)), dma((1,)), dma((3,)),
         ],
         compiler_params=pltpu.CompilerParams(
             collective_id=0, has_side_effects=True, vmem_limit_bytes=60 * 1024 * 1024
         ),
         name="crosscoder_step",
     )(acts.reshape(TILE, width), weight, enc_bias.reshape(1, nlat), dec_bias)
+    cols = nlat // 2
+    grad_weight, grad_enc, grad_dec = pl.pallas_call(
+        last_product,
+        out_shape=(
+            jax.ShapeDtypeStruct((2, width, nlat), BF16),
+            jax.ShapeDtypeStruct((1, nlat), F32),
+            jax.ShapeDtypeStruct((2, width), F32),
+        ),
+        grid=(2, 2),
+        in_specs=[
+            pl.BlockSpec((1, width, cols), lambda m, n: (m, 0, n)),
+            pl.BlockSpec((1, width, below), lambda m, n: (m, 0, 0)),
+            pl.BlockSpec((below, cols), lambda m, n: (0, n)),
+            pl.BlockSpec((1, nlat), lambda m, n: (0, 0)),
+            pl.BlockSpec((2, width), lambda m, n: (0, 0)),
+        ],
+        out_specs=(
+            pl.BlockSpec((1, width, cols), lambda m, n: (m, 0, n)),
+            pl.BlockSpec((1, nlat), lambda m, n: (0, 0)),
+            pl.BlockSpec((2, width), lambda m, n: (0, 0)),
+        ),
+        name="last_product",
+    )(acc, xt, grads.reshape(below, nlat), geb, gdb)
     return grad_weight, grad_enc.reshape(nlat), grad_dec
 
 

time: 141 us -> 140 us (level)
  local copies, waits for them, and re-layouts: 4.28 us -> 0 us
  Pallas kernels: 135 us -> 139 us
    pallas_call x0 -> x1, Pallas kernels: none -> 4.97 us  [on_device(): pl.pallas_call(last_product, out_shape=(jax.ShapeDtypeStruct((2, width, n...]
    unnamed x7 -> x0, local copies, waits for them, and re-layouts: 4.28 us -> none
    pallas_call x1, Pallas kernels: 135 us -> 134 us  [on_device(): pl.pallas_call(functools.partial(chain_kernel, sizes, scale), out_shape=(...]
where the time goes in v5:
time: 140 us
  Pallas kernels  139 us (99%)
    pallas_call x1, Pallas kernels, on_device(): pl.pallas_call(functools.partial(chain_kernel, sizes, scale), out_shape=(...  134 us
    pallas_call x1, Pallas kernels, on_device(): pl.pallas_call(last_product, out_shape=(jax.ShapeDtypeStruct((2, width, n...  4.97 us

profile of v5, /device:TPU:1, one launch (start us, length us, event | category | flops | bytes accessed | tf_op | source)
XLA Modules:
  0.0 139.6 jit_solution(3143122262844477084)
XLA Ops:
  0.6 134.0 %crosscoder_step.1 = (f32[2,512,1024]{2,1,0:T(8,128)}, bf16[2,512,256]{2,1,0:T(8,128)(2,1)}, bf16[16,16,1024]{2,1,0:T(8,128)(2,1)}, f32[1,1024]{1,0:T(1,128)}, f32[2,512]{1,0:T(2,128)}) custom-call(bf16[16,512]{1,0:T(8,128)(2,1)} %bitcast.5, bf16[2,512,1024]{2,1,0:T(8,128)(2,1)} %w_hbm.1, f32[1,1024]{1,0:T(1,128)} %bitcast.6, f32[2,512]{1,0:T(2,128)} %db_ref.1), custom_call_target="tpu_custom_call" | custom-call | tf_op jit(solution)/shard_map/crosscoder_step/pallas_call | solution.py:450
  134.7 5.0 %last_product.1 = (bf16[2,512,1024]{2,1,0:T(8,128)(2,1)}, f32[1,1024]{1,0:T(1,128)}, f32[2,512]{1,0:T(2,128)}) custom-call(f32[2,512,1024]{2,1,0:T(8,128)} %get-tuple-element.11.acc_ref, bf16[2,512,256]{2,1,0:T(8,128)(2,1)} %get-tuple-element.12.xt_ref, bf16[256,1024]{1,0:T(8,128)(2,1)} %bitcast.4, f32[1,1024]{1,0:T(1,128)} %get-tuple-element.14.geb_in, ...), custom_call_target="tpu_custom_call" | custom-call | tf_op jit(solution)/shard_map/last_product/pallas_call | solution.py:476
